TPU v7x, 256 devices: a whole 4x4x8 slice. The times are simulated.
256 devices in a mesh: island: 8 (over y, x_lo), fsdp: 32 (over z, x_hi, core).
Axes of the slice: x: 4 (x_hi: 2, x_lo: 2; x = x_hi * 2 + x_lo), y: 4, z: 8, core: 2. Of those that a mesh axis runs over, the one named last changes fastest.
Arguments:
- tokens: bfloat16 [65536, 4096], P(('island', 'fsdp')), may hold values from -6 to 6
- upstream: bfloat16 [65536, 1024], P(('island', 'fsdp')), may hold values from -6 to 6
- params: float32 [4096, 1024], P('fsdp'), may hold values from -6 to 6
- momentum: float32 [4096, 1024], P('fsdp'), may hold values from -4 to 4
- projection: float32 [1024, 512], replicated, may hold values from -6 to 6
Outputs:
- values: bfloat16 [65536, 1024], P(('island', 'fsdp'))
- token_grads: bfloat16 [65536, 4096], P(('island', 'fsdp'))
- new_params: float32 [4096, 1024], P('fsdp')
- new_momentum: float32 [4096, 1024], P('fsdp')
All inputs are finite; a program needn't handle non-finite values.
Results may differ from a plain program's by a relative error of at most 0.012.
Values may be sent and summed in bfloat16 or wider, within the bound.
No kernel may reach another device: no remote copies, remote signals or barrier semaphores. Data moves between devices by JAX's collectives and lax.ppermute only.
A program may use at most 128 MiB of HBM per device.

v0:
```python
import math
import jax
import jax.numpy as jnp
from jax import lax
from jax.sharding import PartitionSpec as P


def local(tokens, upstream, params, momentum, projection):
    half_weight = params.astype(jnp.bfloat16)
    inv_width = 1.0 / math.sqrt(tokens.shape[1])
    dims_feat = (((1,), (1,)), ((), ()))
    dims_rows = (((0,), (0,)), ((), ()))
    forward_sum = jnp.dot(
        tokens,
        lax.all_gather(half_weight, "fsdp", axis=0, tiled=True),
        preferred_element_type=jnp.float32,
    )
    product = lax.dot_general(
        upstream,
        lax.all_gather(half_weight, "fsdp", axis=0, tiled=True),
        dims_feat,
        preferred_element_type=jnp.float32,
    )
    token_grads = (product * inv_width).astype(jnp.bfloat16)
    values = (forward_sum * inv_width).astype(jnp.bfloat16)
    fsdp_count = lax.axis_size("fsdp")
    scale_tok = 1.0 / math.sqrt(tokens.shape[0] * fsdp_count)
    local_grad = lax.dot_general(tokens, upstream, dims_rows, preferred_element_type=jnp.float32)
    shard_grad = lax.psum_scatter(local_grad, "fsdp", scatter_dimension=0, tiled=True) * scale_tok
    compressed = jnp.dot(shard_grad, projection, precision=lax.Precision.HIGHEST)
    island_total = lax.psum(compressed.astype(jnp.bfloat16), "island").astype(jnp.float32)
    outer = jnp.dot(island_total, projection.T, precision=lax.Precision.HIGHEST) / (
        projection.shape[1] * lax.axis_size("island")
    )
    new_momentum = 0.9 * momentum + outer
    new_params = params - 0.7 * (outer + 0.9 * new_momentum)
    return (values, token_grads, new_params, new_momentum)


def solution(mesh):
    in_specs = (
        P(("island", "fsdp"), None),
        P(("island", "fsdp"), None),
        P("fsdp", None),
        P("fsdp", None),
        P(),
    )
    out_specs = (
        P(("island", "fsdp"), None),
        P(("island", "fsdp"), None),
        P("fsdp", None),
        P("fsdp", None),
    )
    return jax.shard_map(local, mesh=mesh, in_specs=in_specs, out_specs=out_specs, check_vma=False)
```

profile of v0, /device:TPU:1, one launch (start us, length us, event | category | flops | bytes accessed | tf_op | source)
XLA Modules:
  0.0 444.7 jit_solution(7758417855345706923)
XLA Ops:
  7.2 0.0 copy-start
  7.2 0.0 reduce-scatter.2.cloned.1.call-start
  7.2 1.5 copy-done
  8.8 9.2 %fusion.5 = f32[4096,1024]{1,0:T(8,128)} fusion(bf16[256,4096]{1,0:T(8,128)(2,1)S(1)} %copy-done, bf16[256,1024]{1,0:T(8,128)(2,1)} %param.6), kind=kOutput, calls=%fused_computation.11 | convolution fusion | flops 2147483648 | bytes 19398656 | tf_op jit(solution)/shard_map/dot_general | solution.py:28
  17.9 0.0 reduce-scatter.2.cloned.1.call-update
  17.9 0.0 copy-start.1
  18.0 0.0 copy-start.2
  18.0 0.0 all-reduce.2.cloned.1.call-start
  18.0 219.4 %reduce-scatter.2.cloned.1.call-done = f32[128,1024]{1,0:T(8,128)} async-done(((f32[4096,1024]{1,0:T(8,128)}), f32[128,1024]{1,0:T(8,128)}) %reduce-scatter.2.cloned.1.call-update) | async-done | bytes 524304 | tf_op jit(solution)/shard_map/reduce_scatter | solution.py:29
  237.4 3.7 convolution_convert_fusion
  241.1 0.0 all-reduce.2.cloned.1.call-update
  241.1 0.0 all-gather.2.cloned.1.call-start
  241.2 76.1 %all-reduce.2.cloned.1.call-done = bf16[128,512]{1,0:T(8,128)(2,1)} async-done(((bf16[128,512]{1,0:T(8,128)(2,1)}), bf16[128,512]{1,0:T(8,128)(2,1)}) %all-reduce.2.cloned.1.call-update) | async-done | bytes 131088 | tf_op jit(solution)/shard_map/psum | solution.py:31
  317.3 0.0 copy-done.1
  317.3 0.0 copy-done.2
  317.3 4.0 multiply_subtract_fusion
  321.3 0.0 all-gather.2.cloned.1.call-update
  321.4 0.0 copy-start.3
  321.4 106.3 %all-gather.2.cloned.1.call-done = bf16[4096,1024]{1,0:T(8,128)(2,1)} async-done(((bf16[128,1024]{1,0:T(8,128)(2,1)}), bf16[4096,1024]{1,0:T(8,128)(2,1)}) %all-gather.2.cloned.1.call-update) | async-done | bytes 8388624 | tf_op jit(solution)/shard_map/all_gather | solution.py:15
  427.7 0.0 copy-start.4
  427.7 6.7 %fusion.1 = bf16[256,1024]{1,0:T(8,128)(2,1)} fusion(bf16[256,4096]{1,0:T(8,128)(2,1)S(1)} %copy-done, bf16[4096,1024]{1,0:T(8,128)(2,1)} %all-gather.2.cloned.1.call-done), kind=kOutput, calls=%fused_computation.3 | convolution fusion | flops 2148007936 | bytes 11010048 | tf_op jit(solution)/shard_map/dot_general | solution.py:13
  434.4 0.0 copy-done.3
  434.4 0.0 copy-done.4
  434.4 3.8 fusion
Async XLA Ops:
  7.2 1.6 copy-start
  7.2 230.2 %reduce-scatter.2.cloned.1.call-start = ((), (), s32[]{:S(2)}) async-start(), calls=%async_computation.2 | async-start | bytes 17301504 | tf_op jit(solution)/shard_map/reduce_scatter | solution.py:29
  17.9 299.3 %copy-start.1 = (f32[128,1024]{1,0:T(8,128)S(1)}, f32[128,1024]{1,0:T(8,128)}, u32[]{:S(2)}) copy-start(f32[128,1024]{1,0:T(8,128)} %param.7) | copy-start | bytes 1572868
  18.0 299.3 %copy-start.2 = (f32[128,1024]{1,0:T(8,128)S(1)}, f32[128,1024]{1,0:T(8,128)}, u32[]{:S(2)}) copy-start(f32[128,1024]{1,0:T(8,128)} %param.8) | copy-start | bytes 1572868
  18.0 299.3 %all-reduce.2.cloned.1.call-start = ((), (), s32[]{:S(2)}) async-start(), calls=%async_computation.3 | async-start | bytes 262144 | tf_op jit(solution)/shard_map/psum | solution.py:31
  241.1 186.6 %all-gather.2.cloned.1.call-start = ((), (), s32[]{:S(2)}) async-start(), calls=%async_computation.1 | async-start | bytes 8650752 | tf_op jit(solution)/shard_map/all_gather | solution.py:15
  321.4 113.0 %copy-start.3 = (bf16[256,1024]{1,0:T(8,128)(2,1)S(1)}, bf16[256,1024]{1,0:T(8,128)(2,1)}, u32[]{:S(2)}) copy-start(bf16[256,1024]{1,0:T(8,128)(2,1)} %param.6) | copy-start | bytes 1572868
  427.7 6.7 %copy-start.4 = (bf16[4096,1024]{1,0:T(8,128)(2,1)S(1)}, bf16[4096,1024]{1,0:T(8,128)(2,1)}, u32[]{:S(2)}) copy-start(bf16[4096,1024]{1,0:T(8,128)(2,1)} %all-gather.2.cloned.1.call-done) | copy-start | bytes 25165828
Sparse Core Ops, SparseCore 0:
  18.1 219.2 reduce-scatter.1
  241.3 75.9 all-reduce.1
  321.5 106.1 all-gather.1
where the time goes:
time: 445 us
  waiting for transfers between devices  402 us (90%)
  matrix products  27.4 us (6%)
  between operations  13.8 us (3%)
    reduce_scatter x1, waiting for transfers between devices, local(): lax.psum_scatter(local_grad, 'fsdp', scatter_dimension=0, tiled=True)  219 us
    all_gather x1, waiting for transfers between devices, local(): lax.all_gather(half_weight, 'fsdp', axis=0, tiled=True)  106 us
    psum x1, waiting for transfers between devices, local(): lax.psum(compressed.astype(jnp.bfloat16), 'island').astype(jnp.float32)  76.1 us
    dot_general x1, matrix products, local(): lax.dot_general(tokens, upstream, dims_rows, preferred_element_type=jnp.f...  9.16 us
  transfers between devices with their start and end apart: 3, of which 3 were waited for; matrix products, arithmetic and copies ran while one was open for 0% of the time, Pallas kernels for 0%

commit v1 on v0

--- a/solution.py
+++ b/solution.py
@@ -12,7 +12,9 @@
     dims_rows = (((0,), (0,)), ((), ()))
     forward_sum = jnp.dot(
         tokens,
-        lax.all_gather(half_weight, "fsdp", axis=0, tiled=True),
+        jnp.concatenate(
+            lax.all_to_all(jnp.stack([half_weight] * lax.axis_size("fsdp")), "fsdp", 0, 0), axis=0
+        ),
         preferred_element_type=jnp.float32,
     )
     product = lax.dot_general(

time: 445 us -> 575 us (1.29)
  waiting for transfers between devices: 402 us -> 507 us
  starting transfers between devices: 0.12 us -> 15.3 us
    all_to_all x0 -> x1, waiting for transfers between devices: none -> 211 us  [local(): lax.all_to_all(jnp.stack([half_weight] * lax.axis_size('fsdp')), 'fsdp',...]
    all_gather x1, waiting for transfers between devices: 106 us -> 0.01 us  [local(): lax.all_gather(half_weight, 'fsdp', axis=0, tiled=True)]
    all_to_all x0 -> x1, starting transfers between devices: none -> 15.2 us  [local(): lax.all_to_all(jnp.stack([half_weight] * lax.axis_size('fsdp')), 'fsdp',...]
  transfers between devices with their start and end apart: 3 -> 4, of which waited for: 3 -> 3; matrix products, arithmetic and copies ran while one was open for 0% -> 1% of each run, Pallas kernels for 0% -> 0%
where the time goes in v1:
time: 575 us; the launch traced here: 573 us
  waiting for transfers between devices  507 us (88%)
  matrix products  30.5 us (5%)
  starting transfers between devices  15.3 us (3%)
  between operations  13.8 us (2%)
  local copies, waits for them, and re-layouts  5.85 us (1%)
    reduce_scatter x1, waiting for transfers between devices, local(): lax.psum_scatter(local_grad, 'fsdp', scatter_dimension=0, tiled=True)  219 us
    all_to_all x1, waiting for transfers between devices, local(): lax.all_to_all(jnp.stack([half_weight] * lax.axis_size('fsdp')), 'fsdp',...  211 us
    psum x1, waiting for transfers between devices, local(): lax.psum(compressed.astype(jnp.bfloat16), 'island').astype(jnp.float32)  76.1 us
    all_to_all x1, starting transfers between devices, local(): lax.all_to_all(jnp.stack([half_weight] * lax.axis_size('fsdp')), 'fsdp',...  15.2 us
  transfers between devices with their start and end apart: 4, of which 3 were waited for; matrix products, arithmetic and copies ran while one was open for 1% of the time, Pallas kernels for 0%

profile of v1, /device:TPU:1, one launch (start us, length us, event | category | flops | bytes accessed | tf_op | source)
XLA Modules:
  0.0 573.0 jit_solution(2527498018438119255)
XLA Ops:
  7.2 0.0 copy-start
  7.2 0.0 reduce-scatter.2.cloned.1.call-start
  7.2 1.5 copy-done
  8.8 9.2 %fusion.5 = f32[4096,1024]{1,0:T(8,128)} fusion(bf16[256,4096]{1,0:T(8,128)(2,1)S(1)} %copy-done, bf16[256,1024]{1,0:T(8,128)(2,1)} %param.6), kind=kOutput, calls=%fused_computation.11 | convolution fusion | flops 2147483648 | bytes 19398656 | tf_op jit(solution)/shard_map/dot_general | solution.py:30
  17.9 0.0 reduce-scatter.2.cloned.1.call-update
  18.0 0.0 copy-start.2
  18.0 0.0 copy-start.3
  18.0 0.0 all-reduce.2.cloned.1.call-start
  18.0 219.4 %reduce-scatter.2.cloned.1.call-done = f32[128,1024]{1,0:T(8,128)} async-done(((f32[4096,1024]{1,0:T(8,128)}), f32[128,1024]{1,0:T(8,128)}) %reduce-scatter.2.cloned.1.call-update) | async-done | bytes 524304 | tf_op jit(solution)/shard_map/reduce_scatter | solution.py:31
  237.4 3.7 convolution_convert_fusion
  241.1 0.0 all-reduce.2.cloned.1.call-update
  241.2 76.1 %all-reduce.2.cloned.1.call-done = bf16[128,512]{1,0:T(8,128)(2,1)} async-done(((bf16[128,512]{1,0:T(8,128)(2,1)}), bf16[128,512]{1,0:T(8,128)(2,1)}) %all-reduce.2.cloned.1.call-update) | async-done | bytes 131088 | tf_op jit(solution)/shard_map/psum | solution.py:33
  317.3 0.0 copy-done.2
  317.3 0.0 copy-done.3
  317.3 4.0 multiply_subtract_fusion
  321.3 0.0 copy-start.1
  321.3 4.3 stack.2
  325.6 0.0 copy-done.1
  325.6 15.2 %all-to-all-start = ((bf16[32,128,1024]{2,1,0:T(8,128)(2,1)}), bf16[32,128,1024]{2,1,0:T(8,128)(2,1)}, u32[]{:S(2)}, u32[]{:S(2)}) async-start(bf16[32,128,1024]{2,1,0:T(8,128)(2,1)} %stack.2), calls=%async_computation | async-start | bytes 16777216 | tf_op jit(solution)/shard_map/all_to_all | solution.py:16
  340.8 0.0 all-gather.2.cloned.1.call-start
  340.8 0.7 all-gather.2.cloned.1.call-update
  341.5 211.3 %all-to-all-done = bf16[32,128,1024]{2,1,0:T(8,128)(2,1)} async-done(((bf16[32,128,1024]{2,1,0:T(8,128)(2,1)}), bf16[32,128,1024]{2,1,0:T(8,128)(2,1)}, u32[]{:S(2)}, u32[]{:S(2)}) %all-to-all-start) | async-done | bytes 8388640 | tf_op jit(solution)/shard_map/all_to_all | solution.py:16
  552.8 0.0 copy-start.4
  552.8 6.6 %fusion.1 = bf16[256,1024]{1,0:T(8,128)(2,1)} fusion(bf16[256,4096]{1,0:T(8,128)(2,1)S(1)} %copy-done, bf16[4096,1024]{1,0:T(8,128)(2,1)} %bitcast), kind=kOutput, calls=%fused_computation.3 | convolution fusion | flops 2148007936 | bytes 11010048 | tf_op jit(solution)/shard_map/dot_general | solution.py:13
  559.4 0.0 all-gather.2.cloned.1.call-done
  559.4 0.0 copy-done.4
  559.4 7.1 %fusion = bf16[256,4096]{1,0:T(8,128)(2,1)} fusion(bf16[256,1024]{1,0:T(8,128)(2,1)S(1)} %copy-done.4, bf16[4096,1024]{1,0:T(8,128)(2,1)} %all-gather.2.cloned.1.call-done), kind=kOutput, calls=%fused_computation.1 | convolution fusion | flops 2149580800 | bytes 11010048 | tf_op jit(solution)/shard_map/dot_general | solution.py:20
Async XLA Ops:
  7.2 1.6 copy-start
  7.2 230.2 %reduce-scatter.2.cloned.1.call-start = ((), (), s32[]{:S(2)}) async-start(), calls=%async_computation.3 | async-start | bytes 17301504 | tf_op jit(solution)/shard_map/reduce_scatter | solution.py:31
  18.0 299.3 %copy-start.2 = (f32[128,1024]{1,0:T(8,128)S(1)}, f32[128,1024]{1,0:T(8,128)}, u32[]{:S(2)}) copy-start(f32[128,1024]{1,0:T(8,128)} %param.7) | copy-start | bytes 1572868
  18.0 299.3 %copy-start.3 = (f32[128,1024]{1,0:T(8,128)S(1)}, f32[128,1024]{1,0:T(8,128)}, u32[]{:S(2)}) copy-start(f32[128,1024]{1,0:T(8,128)} %param.8) | copy-start | bytes 1572868
  18.0 299.3 %all-reduce.2.cloned.1.call-start = ((), (), s32[]{:S(2)}) async-start(), calls=%async_computation.4 | async-start | bytes 262144 | tf_op jit(solution)/shard_map/psum | solution.py:33
  321.3 4.3 copy-start.1
  325.6 227.2 %all-to-all-start = ((bf16[32,128,1024]{2,1,0:T(8,128)(2,1)}), bf16[32,128,1024]{2,1,0:T(8,128)(2,1)}, u32[]{:S(2)}, u32[]{:S(2)}) async-start(bf16[32,128,1024]{2,1,0:T(8,128)(2,1)} %stack.2), calls=%async_computation | async-start | bytes 16777216 | tf_op jit(solution)/shard_map/all_to_all | solution.py:16
  340.8 218.6 %all-gather.2.cloned.1.call-start = ((), (), s32[]{:S(2)}) async-start(), calls=%async_computation.2 | async-start | bytes 8650752 | tf_op jit(solution)/shard_map/all_gather | solution.py:22
  552.8 6.6 %copy-start.4 = (bf16[256,1024]{1,0:T(8,128)(2,1)S(1)}, bf16[256,1024]{1,0:T(8,128)(2,1)}, u32[]{:S(2)}) copy-start(bf16[256,1024]{1,0:T(8,128)(2,1)} %param.6) | copy-start | bytes 1572868
Sparse Core Ops, SparseCore 0:
  18.1 219.2 reduce-scatter.1
  241.3 75.9 all-reduce.1
  345.0 162.2 all-gather.1

commit v2 on v0

--- a/solution.py
+++ b/solution.py
@@ -28,7 +28,9 @@
     local_grad = lax.dot_general(tokens, upstream, dims_rows, preferred_element_type=jnp.float32)
     shard_grad = lax.psum_scatter(local_grad, "fsdp", scatter_dimension=0, tiled=True) * scale_tok
     compressed = jnp.dot(shard_grad, projection, precision=lax.Precision.HIGHEST)
-    island_total = lax.psum(compressed.astype(jnp.bfloat16), "island").astype(jnp.float32)
+    island_total = jnp.sum(
+        lax.all_gather(compressed.astype(jnp.bfloat16), "island"), axis=0
+    ).astype(jnp.float32)
     outer = jnp.dot(island_total, projection.T, precision=lax.Precision.HIGHEST) / (
         projection.shape[1] * lax.axis_size("island")
     )

time: 445 us -> 410 us (0.921)
  waiting for transfers between devices: 402 us -> 366 us
    psum x1 -> x0, waiting for transfers between devices: 76.1 us -> none  [local(): lax.psum(compressed.astype(jnp.bfloat16), 'island').astype(jnp.float32)]
    all_gather x0 -> x1, waiting for transfers between devices: none -> 40.1 us  [local(): lax.all_gather(compressed.astype(jnp.bfloat16), 'island')]
where the time goes in v2:
time: 410 us
  waiting for transfers between devices  366 us (89%)
  matrix products  27.3 us (7%)
  between operations  13.8 us (3%)
    reduce_scatter x1, waiting for transfers between devices, local(): lax.psum_scatter(local_grad, 'fsdp', scatter_dimension=0, tiled=True)  219 us
    all_gather x1, waiting for transfers between devices, local(): lax.all_gather(half_weight, 'fsdp', axis=0, tiled=True)  106 us
    all_gather x1, waiting for transfers between devices, local(): lax.all_gather(compressed.astype(jnp.bfloat16), 'island')  40.1 us
    dot_general x1, matrix products, local(): lax.dot_general(tokens, upstream, dims_rows, preferred_element_type=jnp.f...  9.16 us
  transfers between devices with their start and end apart: 3, of which 3 were waited for; matrix products, arithmetic and copies ran while one was open for 0% of the time, Pallas kernels for 0%

profile of v2, /device:TPU:1, one launch (start us, length us, event | category | flops | bytes accessed | tf_op | source)
XLA Modules:
  0.0 410.0 jit_solution(4446546454156979347)
XLA Ops:
  7.2 0.0 copy-start
  7.2 0.0 reduce-scatter.2.cloned.1.call-start
  7.2 1.5 copy-done
  8.8 9.2 %fusion.5 = f32[4096,1024]{1,0:T(8,128)} fusion(bf16[256,4096]{1,0:T(8,128)(2,1)S(1)} %copy-done, bf16[256,1024]{1,0:T(8,128)(2,1)} %param.6), kind=kOutput, calls=%fused_computation.11 | convolution fusion | flops 2147483648 | bytes 19398656 | tf_op jit(solution)/shard_map/dot_general | solution.py:28
  17.9 0.0 reduce-scatter.2.cloned.1.call-update
  17.9 0.0 copy-start.1
  18.0 0.0 copy-start.2
  18.0 0.0 all-gather.6.cloned.1.call-start
  18.0 219.4 %reduce-scatter.2.cloned.1.call-done = f32[128,1024]{1,0:T(8,128)} async-done(((f32[4096,1024]{1,0:T(8,128)}), f32[128,1024]{1,0:T(8,128)}) %reduce-scatter.2.cloned.1.call-update) | async-done | bytes 524304 | tf_op jit(solution)/shard_map/reduce_scatter | solution.py:29
  237.4 3.7 convolution_convert_fusion
  241.1 0.0 all-gather.6.cloned.1.call-update
  241.1 0.0 all-gather.4.cloned.1.call-start
  241.2 40.1 %all-gather.6.cloned.1.call-done = bf16[1024,512]{1,0:T(8,128)(2,1)} async-done(((bf16[128,512]{1,0:T(8,128)(2,1)}), bf16[1024,512]{1,0:T(8,128)(2,1)}) %all-gather.6.cloned.1.call-update) | async-done | bytes 1048592 | tf_op jit(solution)/shard_map/all_gather | solution.py:32
  281.3 1.4 reduce_sum.12
  282.6 0.0 copy-done.1
  282.7 0.0 copy-done.2
  282.7 4.0 multiply_subtract_fusion
  286.6 0.0 all-gather.4.cloned.1.call-update
  286.7 0.0 copy-start.3
  286.7 106.4 %all-gather.4.cloned.1.call-done = bf16[4096,1024]{1,0:T(8,128)(2,1)} async-done(((bf16[128,1024]{1,0:T(8,128)(2,1)}), bf16[4096,1024]{1,0:T(8,128)(2,1)}) %all-gather.4.cloned.1.call-update) | async-done | bytes 8388624 | tf_op jit(solution)/shard_map/all_gather | solution.py:15
  393.0 0.0 copy-start.4
  393.0 6.7 %fusion.1 = bf16[256,1024]{1,0:T(8,128)(2,1)} fusion(bf16[256,4096]{1,0:T(8,128)(2,1)S(1)} %copy-done, bf16[4096,1024]{1,0:T(8,128)(2,1)} %all-gather.4.cloned.1.call-done), kind=kOutput, calls=%fused_computation.3 | convolution fusion | flops 2148007936 | bytes 11010048 | tf_op jit(solution)/shard_map/dot_general | solution.py:13
  399.7 0.0 copy-done.3
  399.7 0.0 copy-done.4
  399.7 3.8 fusion
Async XLA Ops:
  7.2 1.6 copy-start
  7.2 230.2 %reduce-scatter.2.cloned.1.call-start = ((), (), s32[]{:S(2)}) async-start(), calls=%async_computation.2 | async-start | bytes 17301504 | tf_op jit(solution)/shard_map/reduce_scatter | solution.py:29
  17.9 264.7 %copy-start.1 = (f32[128,1024]{1,0:T(8,128)S(1)}, f32[128,1024]{1,0:T(8,128)}, u32[]{:S(2)}) copy-start(f32[128,1024]{1,0:T(8,128)} %param.7) | copy-start | bytes 1572868
  18.0 264.7 %copy-start.2 = (f32[128,1024]{1,0:T(8,128)S(1)}, f32[128,1024]{1,0:T(8,128)}, u32[]{:S(2)}) copy-start(f32[128,1024]{1,0:T(8,128)} %param.8) | copy-start | bytes 1572868
  18.0 263.3 %all-gather.6.cloned.1.call-start = ((), (), s32[]{:S(2)}) async-start(), calls=%async_computation.3 | async-start | bytes 1179648 | tf_op jit(solution)/shard_map/all_gather | solution.py:32
  241.1 151.9 %all-gather.4.cloned.1.call-start = ((), (), s32[]{:S(2)}) async-start(), calls=%async_computation.1 | async-start | bytes 8650752 | tf_op jit(solution)/shard_map/all_gather | solution.py:15
  286.7 113.0 %copy-start.3 = (bf16[256,1024]{1,0:T(8,128)(2,1)S(1)}, bf16[256,1024]{1,0:T(8,128)(2,1)}, u32[]{:S(2)}) copy-start(bf16[256,1024]{1,0:T(8,128)(2,1)} %param.6) | copy-start | bytes 1572868
  393.0 6.7 %copy-start.4 = (bf16[4096,1024]{1,0:T(8,128)(2,1)S(1)}, bf16[4096,1024]{1,0:T(8,128)(2,1)}, u32[]{:S(2)}) copy-start(bf16[4096,1024]{1,0:T(8,128)(2,1)} %all-gather.4.cloned.1.call-done) | copy-start | bytes 25165828
Sparse Core Ops, SparseCore 0:
  18.1 219.2 reduce-scatter.1
  241.3 39.9 all-gather.5
  286.8 106.2 all-gather.3
